TPU v7x, 512 devices: a whole 4x8x8 slice. The times are simulated.
512 devices in a mesh: tm: 16 (over z, core), env: 32 (over x, y).
Axes of the slice: x: 4, y: 8, z: 8, core: 2. Of those that a mesh axis runs over, the one named last changes fastest.
Arguments:
- rewards: float32 [4096, 4096], P('tm', 'env'), may hold values from -6 to 6
- dones: int32 [4096, 4096], P('tm', 'env'), may hold values 0 or 1
- horizon: float32 [4096], P('env'), may hold values from 20 to 8192
- bootstrap: float32 [4096], P('env'), may hold values from -96 to 96
- prior_mean: float32 [1], replicated, may hold values from -240 to 240
- prior_var: float32 [1], replicated, may hold values from 100 to 3000
Outputs:
- scaled_rewards: float32 [4096, 4096], P('tm', 'env')
- scaled_returns: float32 [4096, 4096], P('tm', 'env')
- running_stats: float32 [2], replicated
All inputs are finite; a program needn't handle non-finite values. No bound on the sum of `dones` on one device may be relied on, other than what follows from the above.
Results may differ from a plain program's by a relative error of at most 0.0003.
Values sent between devices are 32-bit elements; how exact they have to be, the bound alone decides.
No kernel may reach another device: no remote copies, remote signals or barrier semaphores. Data moves between devices by JAX's collectives and lax.ppermute only.
A program may use at most 64 MiB of HBM per device.

v0:
```python
import jax
import jax.numpy as jnp
from jax import lax
from jax.sharding import Mesh
from jax.sharding import PartitionSpec as P

TM = ("tm_0", "tm_1")
ENV = ("env_0", "env_1")


def sent_to_all(array, axis):
    count = lax.axis_size(axis)
    return lax.all_to_all(
        jnp.broadcast_to(array[None], (count, *array.shape)), axis, 0, 0, tiled=True
    )


def of_everyone(array, axis):
    everything = sent_to_all(array, axis)
    return jnp.sum(everything, axis=0)


def one_axis_at_a_time(array, axes):
    far, near = axes
    return of_everyone(of_everyone(array, near), far)


def together(arrays, axis):
    ends = [0]
    for a in arrays:
        ends.append(ends[-1] + a.size)
    running = one_axis_at_a_time(jnp.concatenate([a.ravel() for a in arrays]), axis)
    return tuple((running[b:e].reshape(a.shape) for a, b, e in zip(arrays, ends, ends[1:])))


def side_by_side(arrays, axis, dim, along):
    ends, at = ([], 0)
    for a in arrays[:-1]:
        at += a.shape[along]
        ends.append(at)
    both = jnp.concatenate(arrays, axis=along)
    return tuple(jnp.split(lax.all_gather(both, axis, axis=dim, tiled=True), ends, axis=along))


def compose(earlier, later):
    return (later[0] + later[1] * earlier[0], later[1] * earlier[1])


def local_returns(rewards, factor):
    summed, product = lax.associative_scan(compose, (rewards[::-1], factor[::-1]), axis=0)
    return (summed[::-1], product[::-1])


def combine_moments(former, latter):
    merged = former[0] + latter[0]
    delta = latter[1] - former[1]
    new_mean = former[1] + delta * latter[0] / merged
    new_spread = former[2] + latter[2] + delta * delta * former[0] * latter[0] / merged
    return (merged, new_mean, new_spread)


def batch_moments(returns, center, total_entries):
    centered = returns - center
    first_sum, second_sum = together(
        (jnp.sum(centered), jnp.sum(centered * centered)), (("tm_0", "tm_1"), ("env_0", "env_1"))
    )
    entries = jnp.float32(total_entries)
    average = center + first_sum / entries
    spread = second_sum - first_sum * first_sum / entries
    return (entries, average, spread)


def finish(batch, prior_mean, prior_var, total_entries):
    prior_count = jnp.float32(total_entries)
    merged, new_mean, new_spread = combine_moments(
        (prior_count, prior_mean[0], prior_var[0] * prior_count), batch
    )
    variance = new_spread / merged
    inverse = 1.0 / jnp.sqrt(variance + 1e-08)
    return (new_mean, variance, inverse)


def local(rewards, dones, horizon, bootstrap, prior_mean, prior_var):
    discount = 1.0 - 1.0 / horizon
    factor = discount[None, :] * (1.0 - dones.astype(jnp.float32))
    time_blocks = lax.axis_size(TM)
    total_entries = rewards.shape[0] * time_blocks * rewards.shape[1] * lax.axis_size(ENV)
    position = lax.axis_index(TM)
    summed, product = local_returns(rewards, factor)
    first_sum = summed[0]
    first_product = product[0]
    table_sum, table_product = side_by_side((first_sum[None, :], first_product[None, :]), TM, 0, 1)

    def fold_back(index, carried):
        block = time_blocks - 1 - index
        updated = table_sum[block] + table_product[block] * carried
        return jnp.where(block > position, updated, carried)

    arrived = lax.fori_loop(0, time_blocks, fold_back, bootstrap)
    returns = summed + product * arrived[None, :]
    batch = batch_moments(returns, prior_mean[0], total_entries)
    new_mean, variance, inverse = finish(batch, prior_mean, prior_var, total_entries)
    return (rewards * inverse, returns * inverse, jnp.stack([new_mean, variance]))


def solution(mesh):
    finer = Mesh(mesh.devices.reshape(8, 2, 4, 8), ("tm_0", "tm_1", "env_0", "env_1"))
    placed = (P(TM, ENV), P(TM, ENV), P(ENV), P(ENV), P(), P())
    return jax.shard_map(
        local, mesh=finer, in_specs=placed, out_specs=(P(TM, ENV), P(TM, ENV), P()), check_vma=False
    )
```

profile of v0, /device:TPU:1, one launch (start us, length us, event | category | flops | bytes accessed | tf_op | source)
XLA Modules:
  0.0 69.8 jit_solution(8349592909752235508)
XLA Ops:
  0.6 0.0 copy-start
  0.6 0.8 %slice.264 = f32[1,128]{1,0:T(1,128)S(1)} slice(f32[256,128]{1,0:T(8,128)} %param.8), slice={[255:256], [0:128]} | slice | bytes 1024 | tf_op jit(solution)/shard_map/slice | solution.py:50
  1.4 0.9 %slice.269 = f32[128,128]{1,0:T(8,128)S(1)} slice(f32[256,128]{1,0:T(8,128)} %param.8), slice={[0:255:2], [0:128:1]} | slice | bytes 131072 | tf_op jit(solution)/shard_map/slice | solution.py:50
  2.3 0.0 copy-done
  2.3 0.0 copy-start.1
  2.3 0.0 copy-start.3
  2.4 0.7 copy-done.3
  3.0 0.2 copy-done.1
  5.9 0.1 rev.9
  6.0 0.1 rev.8
  6.1 24.5 %all-gather = f32[16,1,256]{2,1,0:T(1,128)S(1)} all-gather(f32[1,1,256]{2,1,0:T(1,128)S(1)} %maximum_bitcast_fusion), channel_id=1, replica_groups=mesh['tm_0'=8,'tm_1'=2,'env_0'=4,'env_1'=8] {'tm_0','tm_1'}, dimensions={0}, use_global_device_ids=true | all-gather | bytes 17408 | tf_op jit(solution)/shard_map/all_gather | solution.py:42
  30.6 0.7 copy-done.2
  31.3 0.7 while.15
  32.0 0.6 subtract_reduce_fusion
  32.6 1.4 %pad_maximum_fusion.14 = f32[2]{0:T(128)S(1)} fusion(f32[1]{0:T(128)} %bitcast.5, f32[1]{0:T(128)} %bitcast.4), kind=kLoop, calls=%fused_computation.52 | loop fusion | flops 2 | bytes 16 | tf_op jit(solution)/shard_map/concatenate | solution.py:32
  34.0 18.1 %all_to_all.12 = f32[32,1,2]{2,1,0:T(1,128)S(1)} all-to-all(f32[32,1,2]{2,1,0:T(1,128)S(1)} %broadcast_in_dim.4), channel_id=1, replica_groups=mesh['tm_0'=8,'tm_1'=2,'env_0'=4,'env_1'=8] {'env_0','env_1'}, dimensions={0} | all-to-all | bytes 512 | tf_op jit(solution)/shard_map/all_to_all | solution.py:13
  52.1 0.1 reduce_sum.38
  52.1 0.6 broadcast_in_dim.5
  52.7 4.9 %all-to-all-start.1 = ((f32[16,1,2]{2,1,0:T(1,128)}), f32[16,1,2]{2,1,0:T(1,128)S(1)}, u32[]{:S(2)}, u32[]{:S(2)}) async-start(f32[16,1,2]{2,1,0:T(1,128)} %broadcast_in_dim.5), calls=%async_computation.1 | async-start | bytes 16384 | tf_op jit(solution)/shard_map/all_to_all | solution.py:13
  58.3 6.3 %all-to-all-done.1 = f32[16,1,2]{2,1,0:T(1,128)S(1)} async-done(((f32[16,1,2]{2,1,0:T(1,128)}), f32[16,1,2]{2,1,0:T(1,128)S(1)}, u32[]{:S(2)}, u32[]{:S(2)}) %all-to-all-start.1) | async-done | bytes 160 | tf_op jit(solution)/shard_map/all_to_all | solution.py:13
  64.6 0.6 fusion.14
  67.9 0.7 broadcast_multiply_fusion.1
  68.5 0.7 broadcast_multiply_fusion
  69.2 0.6 pad_maximum_fusion.15
  (154 shorter events, 1.8 us)
Async XLA Ops:
  0.6 1.7 %copy-start = (f32[256,128]{1,0:T(8,128)S(1)}, f32[256,128]{1,0:T(8,128)}, u32[]{:S(2)}) copy-start(f32[256,128]{1,0:T(8,128)} %param.8) | copy-start | bytes 393220
  2.3 0.9 %copy-start.1 = (s32[256,128]{1,0:T(8,128)S(1)}, s32[256,128]{1,0:T(8,128)}, u32[]{:S(2)}) copy-start(s32[256,128]{1,0:T(8,128)} %param.9) | copy-start | bytes 393220
  2.3 0.7 copy-start.3
  30.6 0.7 copy-start.2
  52.7 11.9 %all-to-all-start.1 = ((f32[16,1,2]{2,1,0:T(1,128)}), f32[16,1,2]{2,1,0:T(1,128)S(1)}, u32[]{:S(2)}, u32[]{:S(2)}) async-start(f32[16,1,2]{2,1,0:T(1,128)} %broadcast_in_dim.5), calls=%async_computation.1 | async-start | bytes 16384 | tf_op jit(solution)/shard_map/all_to_all | solution.py:13
where the time goes:
time: 70.1 us; the launch traced here: 69.8 us
  blocking collectives  42.6 us (61%)
  waiting for transfers between devices  6.33 us (9%)
  local copies, waits for them, and re-layouts  5.53 us (8%)
  between operations  5.32 us (8%)
  starting transfers between devices  4.88 us (7%)
  other arithmetic  4.76 us (7%)
    all_gather x1, blocking collectives, side_by_side(): lax.all_gather(both, axis, axis=dim, tiled=True)  24.5 us
    all_to_all x1, blocking collectives, sent_to_all(): lax.all_to_all(jnp.broadcast_to(array[None], (count, *array.shape)), axis...  18.1 us
    all_to_all x1, waiting for transfers between devices, sent_to_all(): lax.all_to_all(jnp.broadcast_to(array[None], (count, *array.shape)), axis...  6.33 us
    all_to_all x1, starting transfers between devices, sent_to_all(): lax.all_to_all(jnp.broadcast_to(array[None], (count, *array.shape)), axis...  4.88 us
    slice x58, local copies, waits for them, and re-layouts, local_returns(): lax.associative_scan(compose, (rewards[::-1], factor[::-1]), axis=0)  2.4 us
    unnamed x9, local copies, waits for them, and re-layouts  1.51 us
  transfers between devices with their start and end apart: 1, of which 1 were waited for; matrix products, arithmetic and copies ran while one was open for 0% of the time, Pallas kernels for 0%

commit v1 on v0

v1 whole, which is shorter than its diff:
```python
import functools

import jax
import jax.numpy as jnp
from jax import lax
from jax.experimental import pallas as pl
from jax.experimental.pallas import tpu as pltpu
from jax.sharding import PartitionSpec as P

SUB = 8
VMEM = pltpu.VMEM
SMEM = pltpu.SMEM


def in_vmem(array):
    return pltpu.with_memory_space_constraint(array, VMEM)


def exclusive(summed, product):
    row = lax.broadcasted_iota(jnp.int32, summed.shape, 0)
    for shift in (1, 2, 4):
        inside = row < SUB - shift
        later_sum = jnp.where(inside, pltpu.roll(summed, SUB - shift, 0), 0.0)
        later_product = jnp.where(inside, pltpu.roll(product, SUB - shift, 0), 1.0)
        summed = summed + product * later_sum
        product = product * later_product
    inside = row < SUB - 1
    enter_sum = jnp.where(inside, pltpu.roll(summed, SUB - 1, 0), 0.0)
    enter_product = jnp.where(inside, pltpu.roll(product, SUB - 1, 0), 1.0)
    return enter_sum, enter_product, summed[0:1], product[0:1]


def block_kernel(copies, mean_ref, rewards_ref, dones_ref, horizon_ref, sent_ref, enter_ref):
    steps, lanes = rewards_ref.shape[0] // SUB, rewards_ref.shape[1]
    center = mean_ref[0]
    discount = jnp.broadcast_to(1.0 - 1.0 / horizon_ref[...], (SUB, lanes))
    zero = jnp.zeros((SUB, lanes), jnp.float32)
    s, p = zero, zero + 1.0
    q1, p1, qq, qp, pp = zero, zero, zero, zero, zero
    for j in reversed(range(steps)):
        rows = pl.ds(j, SUB, stride=steps)
        factor = discount * (1.0 - dones_ref[rows, :].astype(jnp.float32))
        s = rewards_ref[rows, :] + factor * s
        p = factor * p
        q = s - center
        q1, p1 = q1 + q, p1 + p
        qq, qp, pp = qq + q * q, qp + q * p, pp + p * p
    a, b, block_sum, block_product = exclusive(s, p)
    enter_ref[0], enter_ref[1] = a, b
    rows = [
        block_sum,
        block_product,
        jnp.sum(q1 + a * p1, axis=0, keepdims=True),
        jnp.sum(b * p1, axis=0, keepdims=True),
        jnp.sum(qq + a * (2.0 * qp + a * pp), axis=0, keepdims=True),
        jnp.sum(b * (qp + a * pp), axis=0, keepdims=True),
        jnp.sum(b * b * pp, axis=0, keepdims=True),
        zero[0:1],
    ]
    table = jnp.concatenate(rows, axis=0)
    for k in range(copies):
        sent_ref[k] = table


def fold_kernel(copies, position_ref, tables_ref, bootstrap_ref, sent_ref, arrived_ref):
    blocks, _, lanes = tables_ref.shape
    position = position_ref[0]
    carry = bootstrap_ref[...]
    arrived = carry
    first = jnp.zeros_like(carry)
    second = jnp.zeros_like(carry)
    for k in reversed(range(blocks)):
        row = lambda i: tables_ref[k, i : i + 1, :]
        arrived = jnp.where(position == k, carry, arrived)
        first = first + (row(2) + carry * row(3))
        second = second + (row(4) + carry * (2.0 * row(5) + carry * row(6)))
        carry = row(0) + row(1) * carry
    arrived_ref[...] = arrived
    half = lanes // 2
    first = first + pltpu.roll(first, half, 1)
    second = second + pltpu.roll(second, half, 1)
    lane = lax.broadcasted_iota(jnp.int32, first.shape, 1)
    sent_ref[...] = jnp.broadcast_to(jnp.where(lane < half, first, second), (copies, lanes))


def scale_kernel(
    entries, mean_ref, var_ref, totals_ref, arrived_ref, enter_ref, horizon_ref, rewards_ref, dones_ref,
    out_rewards_ref, out_returns_ref, stats_ref,
):
    steps, lanes = rewards_ref.shape[0] // SUB, rewards_ref.shape[1]
    prior_mean, prior_var = mean_ref[0], var_ref[0]
    total = jnp.sum(totals_ref[...], axis=0, keepdims=True)
    lane = lax.broadcasted_iota(jnp.int32, total.shape, 1)
    first_sum = jnp.sum(jnp.where(lane < lanes // 2, total, 0.0), axis=1, keepdims=True)
    second_sum = jnp.sum(jnp.where(lane < lanes // 2, 0.0, total), axis=1, keepdims=True)
    count = jnp.float32(entries)
    merged = count + count
    delta = first_sum / count
    spread = second_sum - first_sum * delta
    new_mean = prior_mean + delta * count / merged
    new_spread = prior_var * count + spread + delta * delta * count * count / merged
    variance = new_spread / merged
    inverse = 1.0 / jnp.sqrt(variance + 1e-08)
    stats_ref[0] = new_mean[0, 0]
    stats_ref[1] = variance[0, 0]
    scale = jnp.broadcast_to(inverse, (SUB, lanes))
    discount = jnp.broadcast_to(1.0 - 1.0 / horizon_ref[...], (SUB, lanes))
    returns = enter_ref[0] + enter_ref[1] * arrived_ref[...]
    for j in reversed(range(steps)):
        rows = pl.ds(j, SUB, stride=steps)
        reward = rewards_ref[rows, :]
        factor = discount * (1.0 - dones_ref[rows, :].astype(jnp.float32))
        returns = reward + factor * returns
        out_returns_ref[rows, :] = returns * scale
        out_rewards_ref[rows, :] = reward * scale


def local(tm, env, rewards, dones, horizon, bootstrap, prior_mean, prior_var):
    steps, lanes = rewards.shape
    blocks, columns = lax.axis_size(tm), lax.axis_size(env)
    entries = steps * lanes * blocks * columns
    vmem = pl.BlockSpec(memory_space=VMEM)
    smem = pl.BlockSpec(memory_space=SMEM)
    f32 = jnp.float32
    rewards, dones = in_vmem(rewards), in_vmem(dones)
    horizon = horizon[None, :]
    sent, enter = pl.pallas_call(
        functools.partial(block_kernel, blocks),
        out_shape=(VMEM((blocks, SUB, lanes), f32), VMEM((2, SUB, lanes), f32)),
        in_specs=[smem, vmem, vmem, vmem],
        out_specs=(vmem, vmem),
        name="block_maps",
    )(prior_mean, rewards, dones, horizon)
    tables = lax.all_to_all(sent, tm, 0, 0, tiled=True)
    position = lax.axis_index(tm).astype(jnp.int32)[None]
    sent, arrived = pl.pallas_call(
        functools.partial(fold_kernel, columns),
        out_shape=(VMEM((columns, lanes), f32), VMEM((1, lanes), f32)),
        in_specs=[smem, vmem, vmem],
        out_specs=(vmem, vmem),
        name="fold_blocks",
    )(position, in_vmem(tables), bootstrap[None, :])
    totals = lax.all_to_all(sent.reshape(columns, 1, lanes), env, 0, 0, tiled=True)
    return tuple(
        pl.pallas_call(
            functools.partial(scale_kernel, entries),
            out_shape=(
                jax.ShapeDtypeStruct(rewards.shape, f32),
                jax.ShapeDtypeStruct(rewards.shape, f32),
                jax.ShapeDtypeStruct((2,), f32),
            ),
            in_specs=[smem, smem, vmem, vmem, vmem, vmem, vmem, vmem],
            out_specs=(vmem, vmem, smem),
            name="scale",
        )(
            prior_mean, prior_var, in_vmem(totals.reshape(columns, lanes)), in_vmem(arrived), in_vmem(enter),
            horizon, rewards, dones,
        )
    )


def solution(mesh):
    tm, env = mesh.axis_names
    placed = (P(tm, env), P(tm, env), P(env), P(env), P(), P())
    return jax.shard_map(
        functools.partial(local, tm, env),
        mesh=mesh,
        in_specs=placed,
        out_specs=(P(tm, env), P(tm, env), P()),
        check_vma=False,
    )
```

time: 70.1 us -> 46 us (0.66)
  blocking collectives: 42.6 us -> 0 us
  starting transfers between devices: 4.88 us -> 21.6 us
  waiting for transfers between devices: 6.33 us -> 15.8 us
  other arithmetic: 4.76 us -> 0 us
  Pallas kernels: 0 us -> 4.53 us
  local copies, waits for them, and re-layouts: 5.53 us -> 1.81 us
  between operations: 5.32 us -> 1.95 us
    all_gather x1 -> x0, blocking collectives: 24.5 us -> none  [side_by_side(): lax.all_gather(both, axis, axis=dim, tiled=True)]
    all_to_all x1 -> x0, blocking collectives: 18.1 us -> none  [sent_to_all(): lax.all_to_all(jnp.broadcast_to(array[None], (count, *array.shape)), axis...]
    all_to_all x1 -> x2, starting transfers between devices: 4.88 us -> 21.6 us  [the longest x1 12 us: local(): tables = lax.all_to_all(sent, tm, 0, 0, tiled=True)]
    all_to_all x1 -> x2, waiting for transfers between devices: 6.33 us -> 15.8 us  [the longest x1 7.94 us: local(): lax.all_to_all(sent.reshape(columns, 1, lanes), env, 0, 0, tiled=True)]
    pallas_call x0 -> x3, Pallas kernels: none -> 4.53 us  [the longest x1 1.7 us: local(): pl.pallas_call(functools.partial(scale_kernel, entries), out_shape=(jax.S...]
    slice x59 -> x0, local copies, waits for them, and re-layouts: 2.99 us -> none  [the longest x58 2.4 us: local_returns(): lax.associative_scan(compose, (rewards[::-1], factor[::-1]), axis=0)]
    mul x17 -> x0, other arithmetic: 1.49 us -> none  [the longest x1 0.67 us: local(): rewards * inverse]
    concatenate x15 -> x0, other arithmetic: 1.49 us -> none  [the longest x1 1.37 us: together(): jnp.concatenate([a.ravel() for a in arrays])]
  transfers between devices with their start and end apart: 1 -> 2, of which waited for: 1 -> 2; matrix products, arithmetic and copies ran while one was open for 0% -> 0% of each run, Pallas kernels for 0% -> 0%
where the time goes in v1:
time: 46 us; the launch traced here: 45.7 us
  starting transfers between devices  21.6 us (47%)
  waiting for transfers between devices  15.8 us (34%)
  Pallas kernels  4.53 us (10%)
  between operations  1.95 us (4%)
  local copies, waits for them, and re-layouts  1.81 us (4%)
    all_to_all x1, starting transfers between devices, local(): tables = lax.all_to_all(sent, tm, 0, 0, tiled=True)  12 us
    all_to_all x1, starting transfers between devices, local(): lax.all_to_all(sent.reshape(columns, 1, lanes), env, 0, 0, tiled=True)  9.67 us
    all_to_all x1, waiting for transfers between devices, local(): lax.all_to_all(sent.reshape(columns, 1, lanes), env, 0, 0, tiled=True)  7.94 us
    all_to_all x1, waiting for transfers between devices, local(): tables = lax.all_to_all(sent, tm, 0, 0, tiled=True)  7.81 us
    unnamed x6, local copies, waits for them, and re-layouts  1.81 us
    pallas_call x1, Pallas kernels, local(): pl.pallas_call(functools.partial(scale_kernel, entries), out_shape=(jax.S...  1.7 us
    pallas_call x1, Pallas kernels, local(): pl.pallas_call(functools.partial(block_kernel, blocks), out_shape=(VMEM((...  1.46 us
    pallas_call x1, Pallas kernels, local(): pl.pallas_call(functools.partial(fold_kernel, columns), out_shape=(VMEM((...  1.37 us
  transfers between devices with their start and end apart: 2, of which 2 were waited for; matrix products, arithmetic and copies ran while one was open for 0% of the time, Pallas kernels for 0%

profile of v1, /device:TPU:1, one launch (start us, length us, event | category | flops | bytes accessed | tf_op | source)
XLA Modules:
  0.0 45.7 jit_solution(10749773992474022331)
XLA Ops:
  1.3 0.0 copy-start
  1.3 0.9 %copy-done = f32[256,128]{1,0:T(8,128)S(1)} copy-done((f32[256,128]{1,0:T(8,128)S(1)}, f32[256,128]{1,0:T(8,128)}, u32[]{:S(2)}) %copy-start) | copy-done | bytes 131096
  2.2 0.0 copy-start.2
  2.2 0.9 %copy-done.2 = s32[256,128]{1,0:T(8,128)S(1)} copy-done((s32[256,128]{1,0:T(8,128)S(1)}, s32[256,128]{1,0:T(8,128)}, u32[]{:S(2)}) %copy-start.2) | copy-done | bytes 131096
  3.1 1.5 %block_maps.1 = (f32[16,8,128]{2,1,0:T(8,128)}, f32[2,8,128]{2,1,0:T(8,128)S(1)}) custom-call(f32[1]{0:T(128)S(6)} %copy.10.mean_ref, f32[256,128]{1,0:T(8,128)S(1)} %copy-done, s32[256,128]{1,0:T(8,128)S(1)} %copy-done.2, f32[1,128]{1,0:T(1,128)} %bitcast.8), custom_call_target="tpu_custom_call" | custom-call | tf_op jit(solution)/shard_map/block_maps/pallas_call | solution.py:127
  4.6 0.0 copy-start.1
  4.6 12.0 %all-to-all-start = ((f32[16,8,128]{2,1,0:T(8,128)}), f32[16,8,128]{2,1,0:T(8,128)S(1)}, u32[]{:S(2)}, u32[]{:S(2)}) async-start(f32[16,8,128]{2,1,0:T(8,128)} %get-tuple-element.7), calls=%async_computation | async-start | bytes 131072 | tf_op jit(solution)/shard_map/all_to_all | solution.py:134
  16.5 7.8 %all-to-all-done.tables_ref = f32[16,8,128]{2,1,0:T(8,128)S(1)} async-done(((f32[16,8,128]{2,1,0:T(8,128)}), f32[16,8,128]{2,1,0:T(8,128)S(1)}, u32[]{:S(2)}, u32[]{:S(2)}) %all-to-all-start) | async-done | bytes 65568 | tf_op jit(solution)/shard_map/all_to_all | solution.py:134
  24.3 1.4 %fold_blocks.1 = (f32[32,128]{1,0:T(8,128)}, f32[1,128]{1,0:T(1,128)S(1)}) custom-call(s32[1]{0:T(128)} %bitcast.position_ref, f32[16,8,128]{2,1,0:T(8,128)S(1)} %all-to-all-done.tables_ref, f32[1,128]{1,0:T(1,128)} %bitcast.10), custom_call_target="tpu_custom_call" | custom-call | tf_op jit(solution)/shard_map/fold_blocks/pallas_call | solution.py:136
  25.7 9.7 %all-to-all-start.1 = ((f32[32,1,128]{2,1,0:T(1,128)}), f32[32,1,128]{2,1,0:T(1,128)S(1)}, u32[]{:S(2)}, u32[]{:S(2)}) async-start(f32[32,1,128]{2,1,0:T(1,128)} %bitcast.4), calls=%async_computation.1 | async-start | bytes 32768 | tf_op jit(solution)/shard_map/all_to_all | solution.py:143
  36.0 7.9 %all-to-all-done.1 = f32[32,1,128]{2,1,0:T(1,128)S(1)} async-done(((f32[32,1,128]{2,1,0:T(1,128)}), f32[32,1,128]{2,1,0:T(1,128)S(1)}, u32[]{:S(2)}, u32[]{:S(2)}) %all-to-all-start.1) | async-done | bytes 16416 | tf_op jit(solution)/shard_map/all_to_all | solution.py:143
  44.0 0.0 copy-done.1
  44.0 1.7 %scale.1 = (f32[256,128]{1,0:T(8,128)}, f32[256,128]{1,0:T(8,128)}, f32[2]{0:T(128)}) custom-call(f32[1]{0:T(128)S(6)} %copy.10.mean_ref, f32[1]{0:T(128)S(6)} %copy.11.var_ref, f32[32,128]{1,0:T(8,128)S(1)} %bitcast.7, f32[1,128]{1,0:T(1,128)S(1)} %get-tuple-element.9.arrived_ref, f32[2,8,128]{2,1,0:T(8,128)S(1)} %get-tuple-element.10.enter_ref, ...), custom_call_target="tpu_custom_call" | custom-call | tf_op jit(solution)/shard_map/scale/pallas_call | solution.py:145
Async XLA Ops:
  1.3 0.9 %copy-start = (f32[256,128]{1,0:T(8,128)S(1)}, f32[256,128]{1,0:T(8,128)}, u32[]{:S(2)}) copy-start(f32[256,128]{1,0:T(8,128)} %rewards_ref.3) | copy-start | bytes 393220
  2.2 0.9 %copy-start.2 = (s32[256,128]{1,0:T(8,128)S(1)}, s32[256,128]{1,0:T(8,128)}, u32[]{:S(2)}) copy-start(s32[256,128]{1,0:T(8,128)} %dones_ref.3) | copy-start | bytes 393220
  4.6 39.4 %copy-start.1 = (f32[256,128]{1,0:T(8,128)S(1)}, f32[256,128]{1,0:T(8,128)}, u32[]{:S(2)}) copy-start(f32[256,128]{1,0:T(8,128)} %rewards_ref.3) | copy-start | bytes 393220
  4.6 19.8 %all-to-all-start = ((f32[16,8,128]{2,1,0:T(8,128)}), f32[16,8,128]{2,1,0:T(8,128)S(1)}, u32[]{:S(2)}, u32[]{:S(2)}) async-start(f32[16,8,128]{2,1,0:T(8,128)} %get-tuple-element.7), calls=%async_computation | async-start | bytes 131072 | tf_op jit(solution)/shard_map/all_to_all | solution.py:134
  25.7 18.3 %all-to-all-start.1 = ((f32[32,1,128]{2,1,0:T(1,128)}), f32[32,1,128]{2,1,0:T(1,128)S(1)}, u32[]{:S(2)}, u32[]{:S(2)}) async-start(f32[32,1,128]{2,1,0:T(1,128)} %bitcast.4), calls=%async_computation.1 | async-start | bytes 32768 | tf_op jit(solution)/shard_map/all_to_all | solution.py:143

commit v2 on v1

v2 whole, which is shorter than its diff:
```python
import functools

import jax
import jax.numpy as jnp
from jax import lax
from jax.experimental import pallas as pl
from jax.experimental.pallas import tpu as pltpu
from jax.sharding import PartitionSpec as P

SUB = 8
VMEM = pltpu.VMEM
SMEM = pltpu.SMEM


def in_vmem(array):
    return pltpu.with_memory_space_constraint(array, VMEM)


def exclusive(summed, product):
    row = lax.broadcasted_iota(jnp.int32, summed.shape, 0)
    for shift in (1, 2, 4):
        inside = row < SUB - shift
        later_sum = jnp.where(inside, pltpu.roll(summed, SUB - shift, 0), 0.0)
        later_product = jnp.where(inside, pltpu.roll(product, SUB - shift, 0), 1.0)
        summed = summed + product * later_sum
        product = product * later_product
    inside = row < SUB - 1
    enter_sum = jnp.where(inside, pltpu.roll(summed, SUB - 1, 0), 0.0)
    enter_product = jnp.where(inside, pltpu.roll(product, SUB - 1, 0), 1.0)
    return enter_sum, enter_product, summed[0:1], product[0:1]


def block_kernel(
    rewards_hbm, dones_hbm, horizon_hbm, bootstrap_hbm,
    sent_ref, rewards_ref, summed_ref, product_ref, kept_ref,
    dones_ref, horizon_ref, bootstrap_ref, sems,
):
    pairs = (
        (horizon_hbm, horizon_ref), (dones_hbm, dones_ref), (rewards_hbm, rewards_ref),
        (bootstrap_hbm, bootstrap_ref),
    )
    loads = [pltpu.make_async_copy(a, b, sems.at[i]) for i, (a, b) in enumerate(pairs)]
    for load in loads:
        load.start()
    steps, _, lanes = summed_ref.shape
    zero = jnp.zeros((SUB, lanes), jnp.float32)
    s, p = zero, zero + 1.0
    s1, p1, ss, sp, pp = zero, zero, zero, zero, zero
    for load in loads:
        load.wait()
    discount = jnp.broadcast_to(1.0 - 1.0 / horizon_ref[...], (SUB, lanes))
    for j in reversed(range(steps)):
        rows = pl.ds(j, SUB, stride=steps)
        factor = discount * (1.0 - dones_ref[rows, :].astype(jnp.float32))
        s = rewards_ref[rows, :] + factor * s
        p = factor * p
        summed_ref[j], product_ref[j] = s, p
        s1, p1 = s1 + s, p1 + p
        ss, sp, pp = ss + s * s, sp + s * p, pp + p * p
    a, b, block_sum, block_product = exclusive(s, p)
    rows = [
        block_sum,
        block_product,
        jnp.sum(s1 + a * p1, axis=0, keepdims=True),
        jnp.sum(b * p1, axis=0, keepdims=True),
        jnp.sum(ss + a * (2.0 * sp + a * pp), axis=0, keepdims=True),
        jnp.sum(b * (sp + a * pp), axis=0, keepdims=True),
        jnp.sum(b * b * pp, axis=0, keepdims=True),
        zero[0:1],
    ]
    table = jnp.concatenate(rows, axis=0)
    for k in range(sent_ref.shape[0]):
        sent_ref[k] = table
    kept_ref[0], kept_ref[1] = a, b
    kept_ref[2] = jnp.broadcast_to(bootstrap_ref[...], (SUB, lanes))


def fold_kernel(tm, tables_ref, kept_ref, sent_ref, carry_ref):
    blocks, _, lanes = tables_ref.shape
    position = lax.axis_index(tm)
    carry = kept_ref[2, 0:1, :]
    arrived = carry
    first = jnp.zeros_like(carry)
    second = jnp.zeros_like(carry)
    for k in reversed(range(blocks)):
        row = lambda i: tables_ref[k, i : i + 1, :]
        arrived = jnp.where(position == k, carry, arrived)
        first = first + (row(2) + carry * row(3))
        second = second + (row(4) + carry * (2.0 * row(5) + carry * row(6)))
        carry = row(0) + row(1) * carry
    half = lanes // 2
    first = first + pltpu.roll(first, half, 1)
    second = second + pltpu.roll(second, half, 1)
    lane = lax.broadcasted_iota(jnp.int32, first.shape, 1)
    sent_ref[...] = jnp.broadcast_to(jnp.where(lane < half, first, second), sent_ref.shape)
    carry_ref[...] = kept_ref[0] + kept_ref[1] * arrived


def scale_kernel(
    entries, mean_ref, var_ref, totals_ref, carry_ref, rewards_ref, summed_ref, product_ref,
    out_rewards_hbm, out_returns_hbm, stats_hbm, scaled_rewards, scaled_returns, stats, sems,
):
    steps, _, lanes = summed_ref.shape
    prior_mean, prior_var = mean_ref[0:1, 0:1], var_ref[0:1, 0:1]
    total = jnp.sum(totals_ref[...], axis=0, keepdims=True)
    lane = lax.broadcasted_iota(jnp.int32, total.shape, 1)
    first_sum = jnp.sum(jnp.where(lane < lanes // 2, total, 0.0), axis=1, keepdims=True)
    second_sum = jnp.sum(jnp.where(lane < lanes // 2, 0.0, total), axis=1, keepdims=True)
    count = jnp.float32(entries)
    merged = count + count
    average = first_sum / count
    spread = second_sum - first_sum * average
    delta = average - prior_mean
    new_mean = prior_mean + delta * count / merged
    new_spread = prior_var * count + spread + delta * delta * count * count / merged
    variance = new_spread / merged
    inverse = 1.0 / jnp.sqrt(variance + 1e-08)
    scale = jnp.broadcast_to(inverse, (SUB, lanes))
    stores = [
        pltpu.make_async_copy(a, b, sems.at[i])
        for i, (a, b) in enumerate(
            ((scaled_returns, out_returns_hbm), (scaled_rewards, out_rewards_hbm), (stats, stats_hbm))
        )
    ]
    carry = carry_ref[...] * scale
    for j in range(steps):
        scaled_returns[pl.ds(j, SUB, stride=steps), :] = summed_ref[j] * scale + product_ref[j] * carry
    stores[0].start()
    for j in range(steps):
        rows = pl.ds(j * SUB, SUB)
        scaled_rewards[rows, :] = rewards_ref[rows, :] * scale
    stores[1].start()
    stats[0] = new_mean[0, 0]
    stats[1] = variance[0, 0]
    stores[2].start()
    for store in stores:
        store.wait()


def local(tm, env, rewards, dones, horizon, bootstrap, prior_mean, prior_var):
    rows, lanes = rewards.shape
    steps = rows // SUB
    blocks, columns = lax.axis_size(tm), lax.axis_size(env)
    entries = rows * lanes * blocks * columns
    vmem = pl.BlockSpec(memory_space=VMEM)
    hbm = pl.BlockSpec(memory_space=pltpu.HBM)
    f32 = jnp.float32
    sent, rewards_here, summed, product, kept = pl.pallas_call(
        block_kernel,
        out_shape=(
            VMEM((blocks, SUB, lanes), f32),
            VMEM((rows, lanes), f32),
            VMEM((steps, SUB, lanes), f32),
            VMEM((steps, SUB, lanes), f32),
            VMEM((3, SUB, lanes), f32),
        ),
        in_specs=[hbm] * 4,
        out_specs=(vmem,) * 5,
        scratch_shapes=[
            VMEM((rows, lanes), jnp.int32),
            VMEM((1, lanes), f32),
            VMEM((1, lanes), f32),
            pltpu.SemaphoreType.DMA((4,)),
        ],
        name="block_maps",
    )(rewards, dones, horizon[None, :], bootstrap[None, :])
    tables = lax.all_to_all(sent, tm, 0, 0, tiled=True)
    sent, carry = pl.pallas_call(
        functools.partial(fold_kernel, tm),
        out_shape=(VMEM((columns, lanes), f32), VMEM((SUB, lanes), f32)),
        in_specs=[vmem, vmem],
        out_specs=(vmem, vmem),
        name="fold_blocks",
    )(in_vmem(tables), in_vmem(kept))
    totals = lax.all_to_all(sent.reshape(columns, 1, lanes), env, 0, 0, tiled=True)
    totals = totals.reshape(columns, lanes)
    return tuple(
        pl.pallas_call(
            functools.partial(scale_kernel, entries),
            out_shape=(
                jax.ShapeDtypeStruct((rows, lanes), f32),
                jax.ShapeDtypeStruct((rows, lanes), f32),
                jax.ShapeDtypeStruct((2,), f32),
            ),
            in_specs=[vmem] * 7,
            out_specs=(hbm,) * 3,
            scratch_shapes=[
                VMEM((rows, lanes), f32),
                VMEM((rows, lanes), f32),
                SMEM((2,), f32),
                pltpu.SemaphoreType.DMA((3,)),
            ],
            name="scale",
        )(prior_mean[None], prior_var[None], *map(in_vmem, (totals, carry, rewards_here, summed, product)))
    )


def solution(mesh):
    tm, env = mesh.axis_names
    placed = (P(tm, env), P(tm, env), P(env), P(env), P(), P())
    return jax.shard_map(
        functools.partial(local, tm, env),
        mesh=mesh,
        in_specs=placed,
        out_specs=(P(tm, env), P(tm, env), P()),
        check_vma=False,
    )
```

time: 46 us -> 41.5 us (0.902)
  blocking collectives: 0 us -> 19.4 us
  starting transfers between devices: 21.6 us -> 9.67 us
  waiting for transfers between devices: 15.8 us -> 7.3 us
  local copies, waits for them, and re-layouts: 1.81 us -> 0 us
  Pallas kernels: 4.53 us -> 2.92 us
    all_to_all x0 -> x1, blocking collectives: none -> 19.4 us  [local(): tables = lax.all_to_all(sent, tm, 0, 0, tiled=True)]
    all_to_all x1 -> x0, starting transfers between devices: 12 us -> none  [local(): tables = lax.all_to_all(sent, tm, 0, 0, tiled=True)]
    all_to_all x1 -> x0, waiting for transfers between devices: 7.81 us -> none  [local(): tables = lax.all_to_all(sent, tm, 0, 0, tiled=True)]
    unnamed x6 -> x0, local copies, waits for them, and re-layouts: 1.81 us -> none
    pallas_call x2, Pallas kernels: 2.83 us -> 1.92 us  [the longest x1 1.21 us: local(): pl.pallas_call(block_kernel, out_shape=(VMEM((blocks, SUB, lanes), f32),...]
    pallas_call x1, Pallas kernels: 1.7 us -> 1 us  [local(): pl.pallas_call(functools.partial(scale_kernel, entries), out_shape=(jax.S...]
    all_to_all x1, waiting for transfers between devices: 7.94 us -> 7.3 us  [local(): lax.all_to_all(sent.reshape(columns, 1, lanes), env, 0, 0, tiled=True)]
  transfers between devices with their start and end apart: 2 -> 1, of which waited for: 2 -> 1; matrix products, arithmetic and copies ran while one was open for 0% -> 0% of each run, Pallas kernels for 0% -> 0%
where the time goes in v2:
time: 41.5 us; the launch traced here: 41.3 us
  blocking collectives  19.4 us (47%)
  starting transfers between devices  9.67 us (23%)
  waiting for transfers between devices  7.3 us (18%)
  Pallas kernels  2.92 us (7%)
  between operations  1.94 us (5%)
    all_to_all x1, blocking collectives, local(): tables = lax.all_to_all(sent, tm, 0, 0, tiled=True)  19.4 us
    all_to_all x1, starting transfers between devices, local(): lax.all_to_all(sent.reshape(columns, 1, lanes), env, 0, 0, tiled=True)  9.67 us
    all_to_all x1, waiting for transfers between devices, local(): lax.all_to_all(sent.reshape(columns, 1, lanes), env, 0, 0, tiled=True)  7.3 us
    pallas_call x1, Pallas kernels, local(): pl.pallas_call(block_kernel, out_shape=(VMEM((blocks, SUB, lanes), f32),...  1.21 us
    pallas_call x1, Pallas kernels, local(): pl.pallas_call(functools.partial(scale_kernel, entries), out_shape=(jax.S...  1 us
  transfers between devices with their start and end apart: 1, of which 1 were waited for; matrix products, arithmetic and copies ran while one was open for 0% of the time, Pallas kernels for 0%

profile of v2, /device:TPU:1, one launch (start us, length us, event | category | flops | bytes accessed | tf_op | source)
XLA Modules:
  0.0 41.3 jit_solution(1081279543103218387)
XLA Ops:
  0.6 1.2 %block_maps.1 = (f32[16,8,128]{2,1,0:T(8,128)S(1)}, f32[256,128]{1,0:T(8,128)S(1)}, f32[32,8,128]{2,1,0:T(8,128)S(1)}, f32[32,8,128]{2,1,0:T(8,128)S(1)}, f32[3,8,128]{2,1,0:T(8,128)S(1)}) custom-call(f32[256,128]{1,0:T(8,128)} %rewards_hbm.1, s32[256,128]{1,0:T(8,128)} %dones_hbm.1, f32[1,128]{1,0:T(1,128)} %bitcast.11, f32[1,128]{1,0:T(1,128)} %bitcast.12), custom_call_target="tpu_custom_call" | custom-call | tf_op jit(solution)/shard_map/block_maps/pallas_call | solution.py:148
  1.8 19.4 %all_to_all.10.tables_ref = f32[16,8,128]{2,1,0:T(8,128)S(1)} all-to-all(f32[16,8,128]{2,1,0:T(8,128)S(1)} %get-tuple-element.10), channel_id=1, replica_groups=mesh['tm'=16,'env'=32] {'tm'}, dimensions={0} | all-to-all | bytes 131072 | tf_op jit(solution)/shard_map/all_to_all | solution.py:167
  21.3 0.7 %fold_blocks.1 = (f32[32,128]{1,0:T(8,128)}, f32[8,128]{1,0:T(8,128)S(1)}) custom-call(f32[16,8,128]{2,1,0:T(8,128)S(1)} %all_to_all.10.tables_ref, f32[3,8,128]{2,1,0:T(8,128)S(1)} %get-tuple-element.11.kept_ref), custom_call_target="tpu_custom_call" | custom-call | tf_op jit(solution)/shard_map/fold_blocks/pallas_call | solution.py:168
  22.0 9.7 %all-to-all-start.1 = ((f32[32,1,128]{2,1,0:T(1,128)}), f32[32,1,128]{2,1,0:T(1,128)S(1)}, u32[]{:S(2)}, u32[]{:S(2)}) async-start(f32[32,1,128]{2,1,0:T(1,128)} %bitcast.5), calls=%async_computation.1 | async-start | bytes 32768 | tf_op jit(solution)/shard_map/all_to_all | solution.py:175
  33.0 7.3 %all-to-all-done.1 = f32[32,1,128]{2,1,0:T(1,128)S(1)} async-done(((f32[32,1,128]{2,1,0:T(1,128)}), f32[32,1,128]{2,1,0:T(1,128)S(1)}, u32[]{:S(2)}, u32[]{:S(2)}) %all-to-all-start.1) | async-done | bytes 16416 | tf_op jit(solution)/shard_map/all_to_all | solution.py:175
  40.3 1.0 %scale.1 = (f32[256,128]{1,0:T(8,128)}, f32[256,128]{1,0:T(8,128)}, f32[2]{0:T(128)}) custom-call(f32[1,1]{1,0:T(1,128)} %bitcast.8.mean_ref, f32[1,1]{1,0:T(1,128)} %bitcast.9.var_ref, f32[32,128]{1,0:T(8,128)S(1)} %bitcast.10, f32[8,128]{1,0:T(8,128)S(1)} %get-tuple-element.13.carry_ref, f32[256,128]{1,0:T(8,128)S(1)} %get-tuple-element.14.rewards_ref, ...), custom_call_target="tpu_custom_call" | custom-call | tf_op jit(solution)/shard_map/scale/pallas_call | solution.py:178
Async XLA Ops:
  22.0 18.3 %all-to-all-start.1 = ((f32[32,1,128]{2,1,0:T(1,128)}), f32[32,1,128]{2,1,0:T(1,128)S(1)}, u32[]{:S(2)}, u32[]{:S(2)}) async-start(f32[32,1,128]{2,1,0:T(1,128)} %bitcast.5), calls=%async_computation.1 | async-start | bytes 32768 | tf_op jit(solution)/shard_map/all_to_all | solution.py:175

commit v3 on v2

--- a/solution.py
+++ b/solution.py
@@ -31,7 +31,7 @@
 
 
 def block_kernel(
-    rewards_hbm, dones_hbm, horizon_hbm, bootstrap_hbm,
+    prior_ref, rewards_hbm, dones_hbm, horizon_hbm, bootstrap_hbm,
     sent_ref, rewards_ref, summed_ref, product_ref, kept_ref,
     dones_ref, horizon_ref, bootstrap_ref, sems,
 ):
@@ -66,7 +66,7 @@
         jnp.sum(ss + a * (2.0 * sp + a * pp), axis=0, keepdims=True),
         jnp.sum(b * (sp + a * pp), axis=0, keepdims=True),
         jnp.sum(b * b * pp, axis=0, keepdims=True),
-        zero[0:1],
+        prior_ref[...],
     ]
     table = jnp.concatenate(rows, axis=0)
     for k in range(sent_ref.shape[0]):
@@ -93,15 +93,17 @@
     second = second + pltpu.roll(second, half, 1)
     lane = lax.broadcasted_iota(jnp.int32, first.shape, 1)
     sent_ref[...] = jnp.broadcast_to(jnp.where(lane < half, first, second), sent_ref.shape)
-    carry_ref[...] = kept_ref[0] + kept_ref[1] * arrived
+    carry_ref[0] = kept_ref[0] + kept_ref[1] * arrived
+    carry_ref[1] = jnp.broadcast_to(tables_ref[0, SUB - 1 : SUB, :], (SUB, lanes))
+    carry_ref[2] = jnp.broadcast_to(tables_ref[1, SUB - 1 : SUB, :], (SUB, lanes))
 
 
 def scale_kernel(
-    entries, mean_ref, var_ref, totals_ref, carry_ref, rewards_ref, summed_ref, product_ref,
+    entries, totals_ref, carry_ref, rewards_ref, summed_ref, product_ref,
     out_rewards_hbm, out_returns_hbm, stats_hbm, scaled_rewards, scaled_returns, stats, sems,
 ):
     steps, _, lanes = summed_ref.shape
-    prior_mean, prior_var = mean_ref[0:1, 0:1], var_ref[0:1, 0:1]
+    prior_mean, prior_var = carry_ref[1, 0:1, 0:1], carry_ref[2, 0:1, 0:1]
     total = jnp.sum(totals_ref[...], axis=0, keepdims=True)
     lane = lax.broadcasted_iota(jnp.int32, total.shape, 1)
     first_sum = jnp.sum(jnp.where(lane < lanes // 2, total, 0.0), axis=1, keepdims=True)
@@ -122,7 +124,7 @@
             ((scaled_returns, out_returns_hbm), (scaled_rewards, out_rewards_hbm), (stats, stats_hbm))
         )
     ]
-    carry = carry_ref[...] * scale
+    carry = carry_ref[0] * scale
     for j in range(steps):
         scaled_returns[pl.ds(j, SUB, stride=steps), :] = summed_ref[j] * scale + product_ref[j] * carry
     stores[0].start()
@@ -145,6 +147,12 @@
     vmem = pl.BlockSpec(memory_space=VMEM)
     hbm = pl.BlockSpec(memory_space=pltpu.HBM)
     f32 = jnp.float32
+    row = lambda scalar: lambda _: jnp.broadcast_to(scalar, (1, lanes))
+    prior = lax.switch(
+        jnp.minimum(lax.axis_index(tm), 2),
+        (row(prior_mean), row(prior_var), lambda _: jnp.zeros((1, lanes), f32)),
+        0,
+    )
     sent, rewards_here, summed, product, kept = pl.pallas_call(
         block_kernel,
         out_shape=(
@@ -154,7 +162,7 @@
             VMEM((steps, SUB, lanes), f32),
             VMEM((3, SUB, lanes), f32),
         ),
-        in_specs=[hbm] * 4,
+        in_specs=[vmem] + [hbm] * 4,
         out_specs=(vmem,) * 5,
         scratch_shapes=[
             VMEM((rows, lanes), jnp.int32),
@@ -163,11 +171,11 @@
             pltpu.SemaphoreType.DMA((4,)),
         ],
         name="block_maps",
-    )(rewards, dones, horizon[None, :], bootstrap[None, :])
+    )(in_vmem(prior), rewards, dones, horizon[None, :], bootstrap[None, :])
     tables = lax.all_to_all(sent, tm, 0, 0, tiled=True)
     sent, carry = pl.pallas_call(
         functools.partial(fold_kernel, tm),
-        out_shape=(VMEM((columns, lanes), f32), VMEM((SUB, lanes), f32)),
+        out_shape=(VMEM((columns, lanes), f32), VMEM((3, SUB, lanes), f32)),
         in_specs=[vmem, vmem],
         out_specs=(vmem, vmem),
         name="fold_blocks",
@@ -182,7 +190,7 @@
                 jax.ShapeDtypeStruct((rows, lanes), f32),
                 jax.ShapeDtypeStruct((2,), f32),
             ),
-            in_specs=[vmem] * 7,
+            in_specs=[vmem] * 5,
             out_specs=(hbm,) * 3,
             scratch_shapes=[
                 VMEM((rows, lanes), f32),
@@ -191,7 +199,7 @@
                 pltpu.SemaphoreType.DMA((3,)),
             ],
             name="scale",
-        )(prior_mean[None], prior_var[None], *map(in_vmem, (totals, carry, rewards_here, summed, product)))
+        )(*map(in_vmem, (totals, carry, rewards_here, summed, product)))
     )
 
 

time: 41.5 us -> 40.7 us (0.981)
  blocking collectives: 19.4 us -> 36.9 us
  starting transfers between devices: 9.67 us -> 0 us
  waiting for transfers between devices: 7.3 us -> 0 us
  between operations: 1.94 us -> 0.66 us
  local copies, waits for them, and re-layouts: 0 us -> 0.65 us
  Pallas kernels: 2.92 us -> 2.28 us
    all_to_all x0 -> x1, blocking collectives: none -> 18.1 us  [local(): lax.all_to_all(sent.reshape(columns, 1, lanes), env, 0, 0, tiled=True)]
    all_to_all x1 -> x0, starting transfers between devices: 9.67 us -> none  [local(): lax.all_to_all(sent.reshape(columns, 1, lanes), env, 0, 0, tiled=True)]
    all_to_all x1 -> x0, waiting for transfers between devices: 7.3 us -> none  [local(): lax.all_to_all(sent.reshape(columns, 1, lanes), env, 0, 0, tiled=True)]
    broadcast_in_dim x0 -> x1, local copies, waits for them, and re-layouts: none -> 0.65 us  [local(): row = lambda scalar: lambda _: jnp.broadcast_to(scalar, (1, lanes))]
    all_to_all x1, blocking collectives: 19.4 us -> 18.8 us  [local(): tables = lax.all_to_all(sent, tm, 0, 0, tiled=True)]
    pallas_call x1, Pallas kernels: 0.71 us -> 0.11 us  [local(): pl.pallas_call(functools.partial(fold_kernel, tm), out_shape=(VMEM((colum...]
  transfers between devices with their start and end apart: 1 -> 0, of which waited for: 1 -> 0; matrix products, arithmetic and copies ran while one was open for 0% -> 0% of each run, Pallas kernels for 0% -> 0%
where the time goes in v3:
time: 40.7 us; the launch traced here: 40.5 us
  blocking collectives  36.9 us (91%)
  Pallas kernels  2.28 us (6%)
  between operations  0.66 us (2%)
  local copies, waits for them, and re-layouts  0.65 us (2%)
    all_to_all x1, blocking collectives, local(): tables = lax.all_to_all(sent, tm, 0, 0, tiled=True)  18.8 us
    all_to_all x1, blocking collectives, local(): lax.all_to_all(sent.reshape(columns, 1, lanes), env, 0, 0, tiled=True)  18.1 us
    pallas_call x1, Pallas kernels, local(): pl.pallas_call(block_kernel, out_shape=(VMEM((blocks, SUB, lanes), f32),...  1.21 us
    pallas_call x1, Pallas kernels, local(): pl.pallas_call(functools.partial(scale_kernel, entries), out_shape=(jax.S...  0.96 us

profile of v3, /device:TPU:1, one launch (start us, length us, event | category | flops | bytes accessed | tf_op | source)
XLA Modules:
  0.0 40.5 jit_solution(13696691197763839688)
XLA Ops:
  0.6 0.7 %conditional.1 = (f32[1,128]{1,0:T(1,128)S(1)}) conditional(s32[]{:T(128)} %clamp.3, (f32[1]{0:T(128)}) %tuple.17, (f32[1]{0:T(128)}) %tuple.18, () %tuple.16), branch_computations={%region_0.0_spmd, %region_1.0_spmd, %region_2.0_spmd} | conditional | bytes 524 | solution.py:151
  0.7 0.6 %broadcast_in_dim.8 = f32[1,128]{1,0:T(1,128)S(1)} broadcast(f32[]{:T(128)} %bitcast.1), dimensions={} | broadcast | bytes 516 | tf_op jit(solution)/shard_map/cond/branch_1_fun/broadcast_in_dim | solution.py:150
  1.3 1.2 %block_maps.1 = (f32[16,8,128]{2,1,0:T(8,128)S(1)}, f32[256,128]{1,0:T(8,128)S(1)}, f32[32,8,128]{2,1,0:T(8,128)S(1)}, f32[32,8,128]{2,1,0:T(8,128)S(1)}, f32[3,8,128]{2,1,0:T(8,128)S(1)}) custom-call(f32[1,128]{1,0:T(1,128)S(1)} %get-tuple-element.27.prior_ref, f32[256,128]{1,0:T(8,128)} %rewards_hbm.1, s32[256,128]{1,0:T(8,128)} %dones_hbm.1, ...), custom_call_target="tpu_custom_call" | custom-call | tf_op jit(solution)/shard_map/block_maps/pallas_call | solution.py:156
  2.5 18.8 %all_to_all.10.tables_ref = f32[16,8,128]{2,1,0:T(8,128)S(1)} all-to-all(f32[16,8,128]{2,1,0:T(8,128)S(1)} %get-tuple-element.16), channel_id=1, replica_groups=mesh['tm'=16,'env'=32] {'tm'}, dimensions={0} | all-to-all | bytes 131072 | tf_op jit(solution)/shard_map/all_to_all | solution.py:175
  21.3 0.1 fold_blocks.1
  21.4 18.1 %all_to_all.11 = f32[32,1,128]{2,1,0:T(1,128)S(1)} all-to-all(f32[32,1,128]{2,1,0:T(1,128)S(1)} %bitcast.9), channel_id=1, replica_groups=mesh['tm'=16,'env'=32] {'env'}, dimensions={0} | all-to-all | bytes 32768 | tf_op jit(solution)/shard_map/all_to_all | solution.py:183
  39.6 1.0 %scale.1 = (f32[256,128]{1,0:T(8,128)}, f32[256,128]{1,0:T(8,128)}, f32[2]{0:T(128)}) custom-call(f32[32,128]{1,0:T(8,128)S(1)} %bitcast.8, f32[3,8,128]{2,1,0:T(8,128)S(1)} %get-tuple-element.19.carry_ref, f32[256,128]{1,0:T(8,128)S(1)} %get-tuple-element.20.rewards_ref, f32[32,8,128]{2,1,0:T(8,128)S(1)} %get-tuple-element.21.summed_ref, ...), custom_call_target="tpu_custom_call" | custom-call | tf_op jit(solution)/shard_map/scale/pallas_call | solution.py:186

commit v4 on v3

--- a/solution.py
+++ b/solution.py
@@ -8,12 +8,18 @@
 from jax.sharding import PartitionSpec as P
 
 SUB = 8
+TM_FIRST, ENV_FIRST = 11, 20
 VMEM = pltpu.VMEM
 SMEM = pltpu.SMEM
 
 
 def in_vmem(array):
     return pltpu.with_memory_space_constraint(array, VMEM)
+
+
+def headed(count, first):
+    first = first % count
+    return [first] + [i for i in range(count) if i != first]
 
 
 def exclusive(summed, product):
@@ -78,12 +84,13 @@
 def fold_kernel(tm, tables_ref, kept_ref, sent_ref, carry_ref):
     blocks, _, lanes = tables_ref.shape
     position = lax.axis_index(tm)
+    order = headed(blocks, TM_FIRST)
     carry = kept_ref[2, 0:1, :]
     arrived = carry
     first = jnp.zeros_like(carry)
     second = jnp.zeros_like(carry)
     for k in reversed(range(blocks)):
-        row = lambda i: tables_ref[k, i : i + 1, :]
+        row = lambda i: tables_ref[order.index(k), i : i + 1, :]
         arrived = jnp.where(position == k, carry, arrived)
         first = first + (row(2) + carry * row(3))
         second = second + (row(4) + carry * (2.0 * row(5) + carry * row(6)))
@@ -94,8 +101,8 @@
     lane = lax.broadcasted_iota(jnp.int32, first.shape, 1)
     sent_ref[...] = jnp.broadcast_to(jnp.where(lane < half, first, second), sent_ref.shape)
     carry_ref[0] = kept_ref[0] + kept_ref[1] * arrived
-    carry_ref[1] = jnp.broadcast_to(tables_ref[0, SUB - 1 : SUB, :], (SUB, lanes))
-    carry_ref[2] = jnp.broadcast_to(tables_ref[1, SUB - 1 : SUB, :], (SUB, lanes))
+    carry_ref[1] = jnp.broadcast_to(tables_ref[order.index(0), SUB - 1 : SUB, :], (SUB, lanes))
+    carry_ref[2] = jnp.broadcast_to(tables_ref[order.index(1), SUB - 1 : SUB, :], (SUB, lanes))
 
 
 def scale_kernel(
@@ -172,7 +179,7 @@
         ],
         name="block_maps",
     )(in_vmem(prior), rewards, dones, horizon[None, :], bootstrap[None, :])
-    tables = lax.all_to_all(sent, tm, 0, 0, tiled=True)
+    tables = lax.all_to_all(sent, tm, 0, 0, tiled=True, axis_index_groups=[headed(blocks, TM_FIRST)])
     sent, carry = pl.pallas_call(
         functools.partial(fold_kernel, tm),
         out_shape=(VMEM((columns, lanes), f32), VMEM((3, SUB, lanes), f32)),
@@ -180,7 +187,7 @@
         out_specs=(vmem, vmem),
         name="fold_blocks",
     )(in_vmem(tables), in_vmem(kept))
-    totals = lax.all_to_all(sent.reshape(columns, 1, lanes), env, 0, 0, tiled=True)
+    totals = lax.all_to_all(sent.reshape(columns, 1, lanes), env, 0, 0, tiled=True, axis_index_groups=[headed(columns, ENV_FIRST)])
     totals = totals.reshape(columns, lanes)
     return tuple(
         pl.pallas_call(

time: 40.7 us -> 32.5 us (0.80)
  blocking collectives: 36.9 us -> 28.7 us
    all_to_all x2, blocking collectives: 36.9 us -> 28.7 us  [the longest x1 16.4 us: local(): lax.all_to_all(sent, tm, 0, 0, tiled=True, axis_index_groups=[headed(bloc...]
where the time goes in v4:
time: 32.5 us; the launch traced here: 32.3 us
  blocking collectives  28.7 us (88%)
  Pallas kernels  2.28 us (7%)
  between operations  0.66 us (2%)
  local copies, waits for them, and re-layouts  0.65 us (2%)
    all_to_all x1, blocking collectives, local(): lax.all_to_all(sent, tm, 0, 0, tiled=True, axis_index_groups=[headed(bloc...  16.4 us
    all_to_all x1, blocking collectives, local(): lax.all_to_all(sent.reshape(columns, 1, lanes), env, 0, 0, tiled=True, ax...  12.3 us
    pallas_call x1, Pallas kernels, local(): pl.pallas_call(block_kernel, out_shape=(VMEM((blocks, SUB, lanes), f32),...  1.21 us
    pallas_call x1, Pallas kernels, local(): pl.pallas_call(functools.partial(scale_kernel, entries), out_shape=(jax.S...  0.96 us

profile of v4, /device:TPU:1, one launch (start us, length us, event | category | flops | bytes accessed | tf_op | source)
XLA Modules:
  0.0 32.3 jit_solution(17476889050531630507)
XLA Ops:
  0.6 0.7 %conditional.1 = (f32[1,128]{1,0:T(1,128)S(1)}) conditional(s32[]{:T(128)} %clamp.3, (f32[1]{0:T(128)}) %tuple.17, (f32[1]{0:T(128)}) %tuple.18, () %tuple.16), branch_computations={%region_0.0_spmd, %region_1.0_spmd, %region_2.0_spmd} | conditional | bytes 524 | solution.py:158
  0.7 0.6 %broadcast_in_dim.8 = f32[1,128]{1,0:T(1,128)S(1)} broadcast(f32[]{:T(128)} %bitcast.1), dimensions={} | broadcast | bytes 516 | tf_op jit(solution)/shard_map/cond/branch_1_fun/broadcast_in_dim | solution.py:157
  1.3 1.2 %block_maps.1 = (f32[16,8,128]{2,1,0:T(8,128)S(1)}, f32[256,128]{1,0:T(8,128)S(1)}, f32[32,8,128]{2,1,0:T(8,128)S(1)}, f32[32,8,128]{2,1,0:T(8,128)S(1)}, f32[3,8,128]{2,1,0:T(8,128)S(1)}) custom-call(f32[1,128]{1,0:T(1,128)S(1)} %get-tuple-element.27.prior_ref, f32[256,128]{1,0:T(8,128)} %rewards_hbm.1, s32[256,128]{1,0:T(8,128)} %dones_hbm.1, ...), custom_call_target="tpu_custom_call" | custom-call | tf_op jit(solution)/shard_map/block_maps/pallas_call | solution.py:163
  2.5 16.4 %all_to_all.10.tables_ref = f32[16,8,128]{2,1,0:T(8,128)S(1)} all-to-all(f32[16,8,128]{2,1,0:T(8,128)S(1)} %get-tuple-element.16), channel_id=1, replica_groups={{352,0,32,64,96,128,160,192,224,256,288,320,384,416,448,480},{353,1,33,..., dimensions={0} | all-to-all | bytes 131072 | tf_op jit(solution)/shard_map/all_to_all | solution.py:182
  19.0 0.1 fold_blocks.1
  19.1 12.3 %all_to_all.11 = f32[32,1,128]{2,1,0:T(1,128)S(1)} all-to-all(f32[32,1,128]{2,1,0:T(1,128)S(1)} %bitcast.9), channel_id=1, replica_groups={{20,0,1,2,3,4,5,6,7,8,9,10,11,12,13,14,15,16,17,18,19,21,22,23,24,25,26..., dimensions={0} | all-to-all | bytes 32768 | tf_op jit(solution)/shard_map/all_to_all | solution.py:190
  31.4 1.0 %scale.1 = (f32[256,128]{1,0:T(8,128)}, f32[256,128]{1,0:T(8,128)}, f32[2]{0:T(128)}) custom-call(f32[32,128]{1,0:T(8,128)S(1)} %bitcast.8, f32[3,8,128]{2,1,0:T(8,128)S(1)} %get-tuple-element.19.carry_ref, f32[256,128]{1,0:T(8,128)S(1)} %get-tuple-element.20.rewards_ref, f32[32,8,128]{2,1,0:T(8,128)S(1)} %get-tuple-element.21.summed_ref, ...), custom_call_target="tpu_custom_call" | custom-call | tf_op jit(solution)/shard_map/scale/pallas_call | solution.py:193
